TPU v7x, 256 devices: a whole 4x4x8 slice. The times are simulated.
256 devices in a mesh: pop: 32 (over x_lo, z, core), tp: 8 (over x_hi, y).
Axes of the slice: x: 4 (x_hi: 2, x_lo: 2; x = x_hi * 2 + x_lo), y: 4, z: 8, core: 2. Of those that a mesh axis runs over, the one named last changes fastest.
Arguments:
- hidden: bfloat16 [2048, 5120], P('pop', 'tp'), may hold values from -24 to 24
- norm_gain: float32 [5120], P('tp'), may hold values from 0.25 to 1.75
- right_factors: bfloat16 [5120, 128], P('tp'), may hold values from -0.078125 to 0.078125
- left_factors: bfloat16 [77824, 128], P(('pop', 'tp')), may hold values from -4 to 4
- targets: int32 [2048], replicated, may hold values from 0 to 77823
- master: float32 [77824, 5120], P(('pop', 'tp')), may hold values from -0.2934839 to 0.2934839
Outputs:
- member_loglik: float32 [64], replicated
- new_master: float32 [77824, 5120], P(('pop', 'tp'))
All inputs are finite; a program needn't handle non-finite values.
Results may differ from a plain program's by a relative error of at most 0.0026.
The roundings to bfloat16 on the way count: a program that leaves them out, or rounds other values in their place, can miss the bound.
Values may be sent and summed in bfloat16 or wider, within the bound.
A program may use at most 128 MiB of HBM per device.

v0:
```python
import jax
import jax.numpy as jnp
from jax import lax
from jax.sharding import PartitionSpec as P

D = 5120
RANK = 4
SEQ = 32
NORM_EPS = 1e-06
SIGMA_NOISE = 0.25
LEARN_RATE = 0.5


def contract(left, right):
    return lax.dot_general(
        left, right, (((1,), (1,)), ((), ())), preferred_element_type=jnp.float32
    )


def body(hidden, norm_gain, right_factors, left_factors, targets, master):
    tok_rows = hidden.shape[0]
    half_rows = tok_rows // 2
    fact_cols = right_factors.shape[1]
    voc_rows = master.shape[0]
    pop_index = lax.axis_index("pop")
    values = hidden.astype(jnp.float32)
    squares = lax.psum(jnp.sum(values * values, axis=1), "tp")
    row_scale = lax.rsqrt(squares / D + NORM_EPS)
    normed = (values * row_scale[:, None] * norm_gain[None, :]).astype(jnp.bfloat16)
    pair_cols = lax.dynamic_slice_in_dim(right_factors, pop_index * RANK, RANK, 1)
    partial_proj = jnp.dot(normed, pair_cols, preferred_element_type=jnp.float32)
    projection = lax.psum(partial_proj, "tp")
    member_sign = jnp.where(jnp.arange(tok_rows) < half_rows, SIGMA_NOISE, -SIGMA_NOISE).astype(
        jnp.float32
    )
    scaled = projection * member_sign[:, None]
    own_block = (lax.iota(jnp.int32, fact_cols) // RANK == pop_index).astype(jnp.float32)
    lowrank = (jnp.tile(scaled, (1, fact_cols // RANK)) * own_block[None, :]).astype(jnp.bfloat16)
    head = master.astype(jnp.bfloat16)
    full_rows, full_right = (
        lax.all_gather(normed, "tp", axis=1, tiled=True),
        lax.all_gather(right_factors, "tp", axis=0, tiled=True),
    )
    joined_rows = jnp.concatenate([full_rows, lowrank], axis=1)
    piece = lax.all_gather(joined_rows, "pop", axis=0, tiled=True)
    logits = contract(piece[:, :D], head) + contract(piece[:, D:], left_factors)
    offset = (pop_index * lax.axis_size("tp") + lax.axis_index("tp")) * voc_rows
    row_max = jnp.max(logits, axis=1)
    column_ids = lax.iota(jnp.int32, voc_rows)
    target_logit = jnp.sum(
        jnp.where(offset + column_ids[None, :] == targets[:, None], logits, 0.0), axis=1
    )
    all_max = lax.pmax(row_max, ("pop", "tp"))
    row_sum = jnp.sum(jnp.exp(logits - all_max[:, None]), axis=1)
    all_sum, all_target = lax.psum((row_sum, target_logit), ("pop", "tp"))
    logprob = all_target - all_max - jnp.log(all_sum)
    member_loglik = jnp.mean(logprob.reshape(-1, SEQ), axis=1)
    fitness = member_loglik[0::2] - member_loglik[1::2]
    weight_cols = jnp.repeat(fitness, RANK)
    scaled_left = (left_factors.astype(jnp.float32) * weight_cols[None, :]).astype(jnp.bfloat16)
    update = contract(scaled_left, full_right)
    new_master = master + LEARN_RATE * update
    return (member_loglik, new_master)


def solution(mesh):
    in_specs = (
        P("pop", "tp"),
        P("tp"),
        P("tp", None),
        P(("pop", "tp"), None),
        P(),
        P(("pop", "tp"), None),
    )
    out_specs = (P(), P(("pop", "tp"), None))
    return jax.shard_map(body, mesh=mesh, in_specs=in_specs, out_specs=out_specs, check_vma=False)
```

profile of v0, /device:TPU:1, one launch (start us, length us, event | category | flops | bytes accessed | tf_op | source)
XLA Modules:
  0.0 395.4 jit_solution(13763955117740881840)
XLA Ops:
  7.2 0.0 copy-start
  7.2 0.0 all-gather.3.cloned.1.call-start
  7.3 1.0 fusion.11
  8.3 21.5 %psum.28 = f32[64]{0:T(128)S(1)} all-reduce(f32[64]{0:T(128)S(1)} %fusion.11), channel_id=1, replica_groups=mesh['pop'=32,'tp'=8] {'tp'}, use_global_device_ids=true, to_apply=%region_1.0 | all-reduce | flops 64 | bytes 512 | tf_op jit(solution)/shard_map/psum | solution.py:27
  29.8 1.0 fusion.13
  30.8 29.9 %all_gather.9 = bf16[64,5120]{1,0:T(8,128)(2,1)S(1)} all-gather(bf16[64,640]{1,0:T(8,128)(2,1)S(1)} %fusion.13), channel_id=1, replica_groups=mesh['pop'=32,'tp'=8] {'tp'}, dimensions={1}, use_global_device_ids=true | all-gather | bytes 737280 | tf_op jit(solution)/shard_map/all_gather | solution.py:41
  60.7 1.2 fusion.14
  61.8 15.7 %psum.29 = f32[64,4]{0,1:T(4,128)S(1)} all-reduce(f32[64,4]{0,1:T(4,128)S(1)} %fusion.14), channel_id=1, replica_groups=mesh['pop'=32,'tp'=8] {'tp'}, use_global_device_ids=true, to_apply=%region_2.0 | all-reduce | flops 256 | bytes 2048 | tf_op jit(solution)/shard_map/psum | solution.py:32
  77.6 0.1 multiply_convert_fusion.2
  77.7 0.1 copy.9
  77.8 0.9 pad_maximum_fusion
  78.7 0.0 all-gather.3.cloned.1.call-update
  78.7 0.0 all-gather.5.cloned.1.call-start
  78.7 0.7 all-gather.5.cloned.1.call-update
  79.5 135.6 %all-gather.3.cloned.1.call-done = bf16[2048,5248]{1,0:T(8,128)(2,1)} async-done(((bf16[64,5248]{1,0:T(8,128)(2,1)}), bf16[2048,5248]{1,0:T(8,128)(2,1)}) %all-gather.3.cloned.1.call-update) | async-done | bytes 21495824 | tf_op jit(solution)/shard_map/all_gather | solution.py:45
  215.0 0.0 copy-done
  215.0 1.5 fusion.9
  216.6 0.0 copy-start.1
  216.6 12.6 %fusion.18 = (f32[2048]{0:T(1024)S(1)}, f32[2048,304]{0,1:T(8,128)S(1)}) fusion(f32[2048,304]{0,1:T(8,128)S(1)} %fusion.9, f32[304,5120]{1,0:T(8,128)} %param.11, bf16[2048,5248]{1,0:T(8,128)(2,1)} %all-gather.3.cloned.1.call-done), kind=kOutput, calls=%fused_computation.33 | convolution fusion | flops 6378141696 | bytes 32186368 | tf_op jit(solution)/shard_map/dot_general | solution.py:15
  229.2 78.5 %pmax.7 = f32[2048]{0:T(1024)S(1)} all-reduce(f32[2048]{0:T(1024)S(1)} %get-tuple-element.6), channel_id=1, replica_groups=mesh['pop'=32,'tp'=8] {'pop','tp'}, use_global_device_ids=true, to_apply=%region_6.7 | all-reduce | flops 2048 | bytes 16384 | tf_op jit(solution)/shard_map/pmax | solution.py:53
  307.8 0.0 copy-done.1
  307.8 0.6 select_reduce_fusion
  308.4 72.7 %all-reduce = (f32[2048]{0:T(1024)S(1)}, f32[2048]{0:T(1024)S(1)}) all-reduce(f32[2048]{0:T(1024)S(1)} %get-tuple-element.3, f32[2048]{0:T(1024)S(1)} %get-tuple-element.2), channel_id=1, replica_groups=mesh['pop'=32,'tp'=8] {'pop','tp'}, use_global_device_ids=true, to_apply=%region_8.9 | all-reduce | flops 4096 | bytes 32768 | tf_op jit(solution)/shard_map/psum | solution.py:55
  381.1 0.1 reshape.41
  381.1 0.1 reduce_sum.39
  381.3 0.0 copy-start.2
  381.3 0.1 slice.14
  381.4 0.1 slice.15
  381.5 0.1 broadcast_in_dim.25
  381.6 0.1 mul.72
  381.7 0.0 all-gather.5.cloned.1.call-done
  381.7 6.8 %fusion.2 = f32[304,5120]{1,0:T(8,128)} fusion(f32[304,5120]{1,0:T(8,128)} %param.11, bf16[5120,128]{1,0:T(8,128)(2,1)} %all-gather.5.cloned.1.call-done, bf16[304,128]{1,0:T(8,128)(2,1)S(1)} %copy-done, f32[128]{0:T(128)S(1)} %mul.72), kind=kOutput, calls=%fused_computation.3 | convolution fusion | flops 401688576 | bytes 13840896 | tf_op jit(solution)/shard_map/dot_general | solution.py:15
  388.6 0.0 copy-done.2
  (9 shorter events, 0.1 us)
Async XLA Ops:
  7.2 207.9 %copy-start = (bf16[304,128]{1,0:T(8,128)(2,1)S(1)}, bf16[304,128]{1,0:T(8,128)(2,1)}, u32[]{:S(2)}) copy-start(bf16[304,128]{1,0:T(8,128)(2,1)} %param.9) | copy-start | bytes 233476
  7.2 207.9 %all-gather.3.cloned.1.call-start = ((), (), s32[]{:S(2)}) async-start(), calls=%async_computation | async-start | bytes 22167552 | tf_op jit(solution)/shard_map/all_gather | solution.py:45
  78.7 303.1 %all-gather.5.cloned.1.call-start = ((), (), s32[]{:S(2)}) async-start(), calls=%async_computation.1 | async-start | bytes 1474560 | tf_op jit(solution)/shard_map/all_gather | solution.py:42
  216.6 91.2 %copy-start.1 = (s32[2048]{0:T(1024)S(1)}, s32[2048]{0:T(1024)}, u32[]{:S(2)}) copy-start(s32[2048]{0:T(1024)} %param.10) | copy-start | bytes 24580
  381.3 7.3 %copy-start.2 = (f32[64]{0:T(128)}, f32[64]{0:T(128)S(1)}, u32[]{:S(2)}) copy-start(f32[64]{0:T(128)S(1)} %broadcast_multiply_fusion.1) | copy-start | bytes 772
Sparse Core Ops, SparseCore 0:
  78.8 136.1 all-gather.2
  217.6 52.0 all-gather.4
where the time goes:
time: 396 us; the launch traced here: 395 us
  blocking collectives  218 us (55%)
  waiting for transfers between devices  136 us (34%)
  matrix products  22.2 us (6%)
  between operations  14.2 us (4%)
    all_gather x1, waiting for transfers between devices, body(): piece = lax.all_gather(joined_rows, 'pop', axis=0, tiled=True)  136 us
    pmax x1, blocking collectives, body(): all_max = lax.pmax(row_max, ('pop', 'tp'))  78.5 us
    psum x1, blocking collectives, body(): all_sum, all_target = lax.psum((row_sum, target_logit), ('pop', 'tp'))  72.7 us
    all_gather x1, blocking collectives, body(): lax.all_gather(normed, 'tp', axis=1, tiled=True)  29.9 us
    psum x1, blocking collectives, body(): squares = lax.psum(jnp.sum(values * values, axis=1), 'tp')  21.5 us
    dot_general x3, matrix products, contract(): lax.dot_general(left, right, (((1,), (1,)), ((), ())), preferred_element_...  21 us
    psum x1, blocking collectives, body(): projection = lax.psum(partial_proj, 'tp')  15.7 us
  transfers between devices with their start and end apart: 2, of which 1 were waited for; matrix products, arithmetic and copies ran while one was open for 4% of the time, Pallas kernels for 0%

commit v1 on v0

--- a/solution.py
+++ b/solution.py
@@ -2,6 +2,7 @@
 import jax.numpy as jnp
 from jax import lax
 from jax.sharding import PartitionSpec as P
+from jax.lax import psum
 
 D = 5120
 RANK = 4
@@ -52,7 +53,11 @@
     )
     all_max = lax.pmax(row_max, ("pop", "tp"))
     row_sum = jnp.sum(jnp.exp(logits - all_max[:, None]), axis=1)
-    all_sum, all_target = lax.psum((row_sum, target_logit), ("pop", "tp"))
+
+    def fill_the_lines(own_rows):
+        return psum(psum(own_rows, "tp"), "pop")
+
+    all_sum, all_target = fill_the_lines((row_sum, target_logit))
     logprob = all_target - all_max - jnp.log(all_sum)
     member_loglik = jnp.mean(logprob.reshape(-1, SEQ), axis=1)
     fitness = member_loglik[0::2] - member_loglik[1::2]

time: 396 us -> 465 us (1.17)
  blocking collectives: 218 us -> 284 us
    psum x1 -> x2, blocking collectives: 72.7 us -> 138 us  [fill_the_lines(): return psum(psum(own_rows, 'tp'), 'pop')]
  transfers between devices with their start and end apart: 2 -> 2, of which waited for: 1 -> 1; matrix products, arithmetic and copies ran while one was open for 4% -> 3% of each run, Pallas kernels for 0% -> 0%
where the time goes in v1:
time: 465 us; the launch traced here: 461 us
  blocking collectives  284 us (61%)
  waiting for transfers between devices  136 us (29%)
  matrix products  22.2 us (5%)
  between operations  14.2 us (3%)
    psum x2, blocking collectives, fill_the_lines(): return psum(psum(own_rows, 'tp'), 'pop')  138 us
    all_gather x1, waiting for transfers between devices, body(): piece = lax.all_gather(joined_rows, 'pop', axis=0, tiled=True)  136 us
    pmax x1, blocking collectives, body(): all_max = lax.pmax(row_max, ('pop', 'tp'))  78.6 us
    all_gather x1, blocking collectives, body(): lax.all_gather(normed, 'tp', axis=1, tiled=True)  29.9 us
    psum x1, blocking collectives, body(): squares = lax.psum(jnp.sum(values * values, axis=1), 'tp')  21.5 us
    dot_general x3, matrix products, contract(): lax.dot_general(left, right, (((1,), (1,)), ((), ())), preferred_element_...  21 us
    psum x1, blocking collectives, body(): projection = lax.psum(partial_proj, 'tp')  15.7 us
  transfers between devices with their start and end apart: 2, of which 1 were waited for; matrix products, arithmetic and copies ran while one was open for 3% of the time, Pallas kernels for 0%

profile of v1, /device:TPU:1, one launch (start us, length us, event | category | flops | bytes accessed | tf_op | source)
XLA Modules:
  0.0 460.9 jit_solution(10950857298111984443)
XLA Ops:
  7.2 0.0 copy-start
  7.2 0.0 all-gather.3.cloned.1.call-start
  7.3 1.0 fusion.11
  8.3 21.5 %psum.42 = f32[64]{0:T(128)S(1)} all-reduce(f32[64]{0:T(128)S(1)} %fusion.11), channel_id=1, replica_groups=mesh['pop'=32,'tp'=8] {'tp'}, use_global_device_ids=true, to_apply=%region_1.0 | all-reduce | flops 64 | bytes 512 | tf_op jit(solution)/shard_map/psum | solution.py:28
  29.8 1.0 fusion.13
  30.8 29.9 %all_gather.9 = bf16[64,5120]{1,0:T(8,128)(2,1)S(1)} all-gather(bf16[64,640]{1,0:T(8,128)(2,1)S(1)} %fusion.13), channel_id=1, replica_groups=mesh['pop'=32,'tp'=8] {'tp'}, dimensions={1}, use_global_device_ids=true | all-gather | bytes 737280 | tf_op jit(solution)/shard_map/all_gather | solution.py:42
  60.7 1.2 fusion.14
  61.8 15.7 %psum.43 = f32[64,4]{0,1:T(4,128)S(1)} all-reduce(f32[64,4]{0,1:T(4,128)S(1)} %fusion.14), channel_id=1, replica_groups=mesh['pop'=32,'tp'=8] {'tp'}, use_global_device_ids=true, to_apply=%region_2.0 | all-reduce | flops 256 | bytes 2048 | tf_op jit(solution)/shard_map/psum | solution.py:33
  77.6 0.1 multiply_convert_fusion.2
  77.7 0.1 copy.9
  77.8 0.9 pad_maximum_fusion
  78.7 0.0 all-gather.3.cloned.1.call-update
  78.7 0.0 all-gather.5.cloned.1.call-start
  78.7 0.7 all-gather.5.cloned.1.call-update
  79.5 135.6 %all-gather.3.cloned.1.call-done = bf16[2048,5248]{1,0:T(8,128)(2,1)} async-done(((bf16[64,5248]{1,0:T(8,128)(2,1)}), bf16[2048,5248]{1,0:T(8,128)(2,1)}) %all-gather.3.cloned.1.call-update) | async-done | bytes 21495824 | tf_op jit(solution)/shard_map/all_gather | solution.py:46
  215.0 0.0 copy-done
  215.0 1.5 fusion.9
  216.6 0.0 copy-start.1
  216.6 12.6 %fusion.18 = (f32[2048]{0:T(1024)S(1)}, f32[2048,304]{0,1:T(8,128)S(1)}) fusion(f32[2048,304]{0,1:T(8,128)S(1)} %fusion.9, f32[304,5120]{1,0:T(8,128)} %param.11, bf16[2048,5248]{1,0:T(8,128)(2,1)} %all-gather.3.cloned.1.call-done), kind=kOutput, calls=%fused_computation.33 | convolution fusion | flops 6378141696 | bytes 32186368 | tf_op jit(solution)/shard_map/dot_general | solution.py:16
  229.2 78.6 %pmax.7 = f32[2048]{0:T(1024)S(1)} all-reduce(f32[2048]{0:T(1024)S(1)} %get-tuple-element.8), channel_id=1, replica_groups=mesh['pop'=32,'tp'=8] {'pop','tp'}, use_global_device_ids=true, to_apply=%region_7.8 | all-reduce | flops 2048 | bytes 16384 | tf_op jit(solution)/shard_map/pmax | solution.py:54
  307.8 0.0 copy-done.1
  307.8 0.6 select_reduce_fusion
  308.4 30.5 %all-reduce.1 = (f32[2048]{0:T(1024)S(1)}, f32[2048]{0:T(1024)S(1)}) all-reduce(f32[2048]{0:T(1024)S(1)} %get-tuple-element.3, f32[2048]{0:T(1024)S(1)} %get-tuple-element.2), channel_id=1, replica_groups=mesh['pop'=32,'tp'=8] {'tp'}, use_global_device_ids=true, to_apply=%region_9.10 | all-reduce | flops 4096 | bytes 32768 | tf_op jit(solution)/shard_map/psum | solution.py:58
  338.9 107.7 %all-reduce = (f32[2048]{0:T(1024)S(1)}, f32[2048]{0:T(1024)S(1)}) all-reduce(f32[2048]{0:T(1024)S(1)} %get-tuple-element.6, f32[2048]{0:T(1024)S(1)} %get-tuple-element.7), channel_id=1, replica_groups=mesh['pop'=32,'tp'=8] {'pop'}, use_global_device_ids=true, to_apply=%region_10.11 | all-reduce | flops 4096 | bytes 32768 | tf_op jit(solution)/shard_map/psum | solution.py:58
  446.6 0.1 reshape.41
  446.6 0.1 reduce_sum.39
  446.8 0.0 copy-start.2
  446.8 0.1 slice.14
  446.9 0.1 slice.15
  447.0 0.1 broadcast_in_dim.25
  447.1 0.1 mul.72
  447.2 0.0 all-gather.5.cloned.1.call-done
  447.3 6.8 %fusion.2 = f32[304,5120]{1,0:T(8,128)} fusion(f32[304,5120]{1,0:T(8,128)} %param.11, bf16[5120,128]{1,0:T(8,128)(2,1)} %all-gather.5.cloned.1.call-done, bf16[304,128]{1,0:T(8,128)(2,1)S(1)} %copy-done, f32[128]{0:T(128)S(1)} %mul.72), kind=kOutput, calls=%fused_computation.3 | convolution fusion | flops 401688576 | bytes 13840896 | tf_op jit(solution)/shard_map/dot_general | solution.py:16
  454.1 0.0 copy-done.2
  (9 shorter events, 0.1 us)
Async XLA Ops:
  7.2 207.9 %copy-start = (bf16[304,128]{1,0:T(8,128)(2,1)S(1)}, bf16[304,128]{1,0:T(8,128)(2,1)}, u32[]{:S(2)}) copy-start(bf16[304,128]{1,0:T(8,128)(2,1)} %param.9) | copy-start | bytes 233476
  7.2 207.9 %all-gather.3.cloned.1.call-start = ((), (), s32[]{:S(2)}) async-start(), calls=%async_computation | async-start | bytes 22167552 | tf_op jit(solution)/shard_map/all_gather | solution.py:46
  78.7 368.6 %all-gather.5.cloned.1.call-start = ((), (), s32[]{:S(2)}) async-start(), calls=%async_computation.1 | async-start | bytes 1474560 | tf_op jit(solution)/shard_map/all_gather | solution.py:43
  216.6 91.2 %copy-start.1 = (s32[2048]{0:T(1024)S(1)}, s32[2048]{0:T(1024)}, u32[]{:S(2)}) copy-start(s32[2048]{0:T(1024)} %param.10) | copy-start | bytes 24580
  446.8 7.3 %copy-start.2 = (f32[64]{0:T(128)}, f32[64]{0:T(128)S(1)}, u32[]{:S(2)}) copy-start(f32[64]{0:T(128)S(1)} %broadcast_multiply_fusion.1) | copy-start | bytes 772
Sparse Core Ops, SparseCore 0:
  78.8 136.1 all-gather.2
  217.6 52.0 all-gather.4
